TPU v7x, 256 devices: a whole 4x4x8 slice. The times are simulated.
256 devices in a mesh: row: 16 (over z, core), col: 16 (over y, x).
Axes of the slice: x: 4, y: 4, z: 8, core: 2. Of those that a mesh axis runs over, the one named last changes fastest.
Arguments:
- inputs: bfloat16 [2048, 8192], P('col', 'row'), may hold values from -6 to 6
- weight: bfloat16 [8192, 28672], P('row', 'col'), may hold values from -0.09375 to 0.09375
- mask: int32 [64, 224], P('row', 'col'), may hold values 0 or 1
- cotangent: bfloat16 [2048, 28672], P('row', 'col'), may hold values from -6 to 6
Outputs:
- outputs: bfloat16 [2048, 28672], P('row', 'col')
- input_grad: bfloat16 [2048, 8192], P('col', 'row')
- weight_grad: bfloat16 [8192, 28672], P('row', 'col')
Inputs may be any that keep to these rules, and one draw needn't show every extreme that they name: mask holds only zeros and ones.
All inputs are finite; a program needn't handle non-finite values. No bound on the sum of `mask` on one device may be relied on, other than what follows from the above.
Results may differ from a plain program's by a relative error of at most 0.022.
Values may be sent and summed in bfloat16 or wider, within the bound.
A program may use at most 128 MiB of HBM per device.

v0:
```python
import jax
import jax.numpy as jnp
from jax import lax
from jax.sharding import PartitionSpec as P

BLOCK = 128


def expand_mask(mask_tile):
    tile_rows, tile_cols = mask_tile.shape
    mask_bf16 = mask_tile.astype(jnp.bfloat16)
    widened = jnp.broadcast_to(mask_bf16[:, None, :, None], (tile_rows, BLOCK, tile_cols, BLOCK))
    return widened.reshape(tile_rows * BLOCK, tile_cols * BLOCK)


def local(inputs, weight, mask, cotangent):
    keep_mask = expand_mask(mask)
    masked = weight * keep_mask
    whole = lax.all_gather(inputs, "col", axis=0, tiled=True)
    token_total = whole.shape[0]
    chosen = whole
    outputs = lax.psum_scatter(
        jnp.dot(chosen, masked, preferred_element_type=jnp.float32).astype(jnp.bfloat16),
        "row",
        scatter_dimension=0,
        tiled=True,
    )
    shard_rows = lax.all_gather(cotangent, "row", axis=0, tiled=True)
    partial_value = lax.dot_general(
        shard_rows, masked, (((1,), (1,)), ((), ())), preferred_element_type=jnp.float32
    )
    grad_parts = partial_value.astype(jnp.bfloat16)
    chosen = whole
    weight_acc = lax.dot_general(
        chosen, shard_rows, (((0,), (0,)), ((), ())), preferred_element_type=jnp.float32
    )
    grad_parts, weight_acc = (grad_parts, weight_acc)
    summed = lax.psum_scatter(
        grad_parts.astype(jnp.float32).astype(jnp.bfloat16), "col", scatter_dimension=0, tiled=True
    )
    grad_scale = token_total ** (-0.5)
    weight_grad = (weight_acc * keep_mask.astype(jnp.float32) * grad_scale).astype(jnp.bfloat16)
    return (outputs, summed, weight_grad)


def solution(mesh):
    placed = (P("col", "row"), P("row", "col"), P("row", "col"), P("row", "col"))
    return jax.shard_map(
        local,
        mesh=mesh,
        in_specs=placed,
        out_specs=(P("row", "col"), P("col", "row"), P("row", "col")),
        check_vma=False,
    )
```

profile of v0, /device:TPU:10, one launch (start us, length us, event | category | flops | bytes accessed | tf_op | source)
XLA Modules:
  0.0 275.3 jit_solution(2744342380747078628)
XLA Ops:
  7.2 0.0 all-gather.5.cloned.1.call-start
  7.2 0.7 all-gather.5.cloned.1.call-update
  7.9 0.0 all-gather.3.cloned.1.call-start
  7.9 0.7 all-gather.3.cloned.1.call-update
  8.6 0.0 reduce-scatter.9.cloned.1.call-start
  8.7 0.7 convert_element_type.23
  9.4 0.1 copy.14
  9.5 3.8 %copy.15 = bf16[512,1792]{0,1:T(8,128)(2,1)} copy(bf16[512,1792]{1,0:T(8,128)(2,1)} %param.5) | data formatting | bytes 3670016 | tf_op args[1]
  13.3 50.4 %all-gather.5.cloned.1.call-done = bf16[2048,1792]{1,0:T(8,128)(2,1)} async-done(((bf16[128,1792]{1,0:T(8,128)(2,1)}), bf16[2048,1792]{1,0:T(8,128)(2,1)}) %all-gather.5.cloned.1.call-update) | async-done | bytes 7340048 | tf_op jit(solution)/shard_map/all_gather | solution.py:28
  63.7 0.5 broadcast_in_dim.2
  64.2 9.1 %fusion.1 = bf16[2048,512]{0,1:T(8,128)(2,1)} fusion(bf16[2048,1792]{1,0:T(8,128)(2,1)} %all-gather.5.cloned.1.call-done, bf16[512,1792]{0,1:T(8,128)(2,1)} %copy.15, bf16[224,8,4,128]{3,2,1,0:T(4,128)(2,1)S(1)} %bitcast.23), kind=kOutput, calls=%fused_computation.4 | convolution fusion | flops 3760062464 | bytes 13107200 | tf_op jit(solution)/shard_map/dot_general | solution.py:29
  73.3 4.0 %copy.21 = bf16[2048,512]{1,0:T(8,128)(2,1)} copy(bf16[2048,512]{0,1:T(8,128)(2,1)} %fusion.1) | data formatting | bytes 4194304
  77.3 0.0 reduce-scatter.9.cloned.1.call-update
  77.3 0.2 reduce-scatter.7.cloned.1.call-start
  77.5 35.6 %all-gather.3.cloned.1.call-done = bf16[2048,512]{1,0:T(8,128)(2,1)} async-done(((bf16[128,512]{1,0:T(8,128)(2,1)}), bf16[2048,512]{1,0:T(8,128)(2,1)}) %all-gather.3.cloned.1.call-update) | async-done | bytes 2097168 | tf_op jit(solution)/shard_map/all_gather | solution.py:19
  113.1 9.1 %fusion = bf16[2048,1792]{0,1:T(8,128)(2,1)} fusion(bf16[2048,512]{1,0:T(8,128)(2,1)} %all-gather.3.cloned.1.call-done, bf16[512,1792]{0,1:T(8,128)(2,1)} %copy.15, bf16[224,8,4,128]{3,2,1,0:T(4,128)(2,1)S(1)} %bitcast.24), kind=kOutput, calls=%fused_computation.1 | convolution fusion | flops 3762683904 | bytes 13107200 | tf_op jit(solution)/shard_map/dot_general | solution.py:23
  122.2 10.1 %copy.19 = bf16[2048,1792]{1,0:T(8,128)(2,1)} copy(bf16[2048,1792]{0,1:T(8,128)(2,1)} %fusion) | data formatting | bytes 14680064
  132.3 0.0 reduce-scatter.7.cloned.1.call-update
  132.3 1.5 copy.31
  133.9 2.8 %copy.16 = bf16[512,1792]{1,0:T(8,128)(2,1)S(1)} copy(bf16[512,1792]{0,1:T(8,128)(2,1)} %bitcast.26) | data formatting | bytes 3670016 | tf_op jit(solution)/shard_map/reshape | solution.py:13
  136.7 9.1 %multiply_convert_fusion = bf16[512,1792]{1,0:T(8,128)(2,1)} fusion(bf16[512,1792]{1,0:T(8,128)(2,1)S(1)} %copy.16, bf16[2048,512]{1,0:T(8,128)(2,1)} %all-gather.3.cloned.1.call-done, bf16[2048,1792]{1,0:T(8,128)(2,1)} %all-gather.5.cloned.1.call-done), kind=kOutput, calls=%fused_computation.2 | convolution fusion | flops 3761766400 | bytes 13107200 | tf_op jit(solution)/shard_map/dot_general | solution.py:34
  145.8 50.3 %reduce-scatter.9.cloned.1.call-done = bf16[128,512]{1,0:T(8,128)(2,1)} async-done(((bf16[2048,512]{1,0:T(8,128)(2,1)}), bf16[128,512]{1,0:T(8,128)(2,1)}) %reduce-scatter.9.cloned.1.call-update) | async-done | bytes 131088
  196.1 72.7 %reduce-scatter.7.cloned.1.call-done = bf16[128,1792]{1,0:T(8,128)(2,1)} async-done(((bf16[2048,1792]{1,0:T(8,128)(2,1)}), bf16[128,1792]{1,0:T(8,128)(2,1)}) %reduce-scatter.7.cloned.1.call-update) | async-done | bytes 458768
Async XLA Ops:
  7.2 56.5 %all-gather.5.cloned.1.call-start = ((), (), s32[]{:S(2)}) async-start(), calls=%async_computation.3 | async-start | bytes 7798784 | tf_op jit(solution)/shard_map/all_gather | solution.py:28
  7.9 105.2 %all-gather.3.cloned.1.call-start = ((), (), s32[]{:S(2)}) async-start(), calls=%async_computation.2 | async-start | bytes 2228224 | tf_op jit(solution)/shard_map/all_gather | solution.py:19
  8.6 187.4 %reduce-scatter.9.cloned.1.call-start = ((), (), s32[]{:S(2)}) async-start(), calls=%async_computation.5 | async-start | bytes 2228224
  77.3 191.5 %reduce-scatter.7.cloned.1.call-start = ((), (), s32[]{:S(2)}) async-start(), calls=%async_computation.4 | async-start | bytes 7798784
Sparse Core Ops, SparseCore 0:
  9.8 53.8 all-gather.4
  66.1 46.9 all-gather.2
  117.3 78.7 reduce-scatter.8
  199.2 69.5 reduce-scatter.6
where the time goes:
time: 276 us; the launch traced here: 275 us
  waiting for transfers between devices  210 us (76%)
  matrix products  27.2 us (10%)
  local copies, waits for them, and re-layouts  22.8 us (8%)
  between operations  13.8 us (5%)
    unnamed x6, waiting for transfers between devices  124 us
    all_gather x1, waiting for transfers between devices, local(): shard_rows = lax.all_gather(cotangent, 'row', axis=0, tiled=True)  50.4 us
    all_gather x1, waiting for transfers between devices, local(): whole = lax.all_gather(inputs, 'col', axis=0, tiled=True)  35.6 us
    unnamed x4, local copies, waits for them, and re-layouts  19.4 us
    dot_general x1, matrix products, local(): jnp.dot(chosen, masked, preferred_element_type=jnp.float32)  9.1 us
    dot_general x1, matrix products, local(): lax.dot_general(chosen, shard_rows, (((0,), (0,)), ((), ())), preferred_e...  9.08 us
    dot_general x1, matrix products, local(): lax.dot_general(shard_rows, masked, (((1,), (1,)), ((), ())), preferred_e...  9.06 us
  transfers between devices with their start and end apart: 4, of which 4 were waited for; matrix products, arithmetic and copies ran while one was open for 18% of the time, Pallas kernels for 0%

commit v1 on v0

--- a/solution.py
+++ b/solution.py
@@ -16,7 +16,21 @@
 def local(inputs, weight, mask, cotangent):
     keep_mask = expand_mask(mask)
     masked = weight * keep_mask
-    whole = lax.all_gather(inputs, "col", axis=0, tiled=True)
+    ways, here, step = (lax.axis_size("col"), lax.axis_index("col"), inputs.shape[0])
+    shape = [n * ways if d == 0 else n for d, n in enumerate(inputs.shape)]
+    full = lax.dynamic_update_slice_in_dim(
+        jnp.zeros(shape, inputs.dtype), inputs, here * step, axis=0
+    )
+    going_up = going_down = inputs
+    for far in range(1, ways // 2 + 1):
+        going_up = lax.ppermute(going_up, "col", [(d, (d + 1) % ways) for d in range(ways)])
+        full = lax.dynamic_update_slice_in_dim(full, going_up, (here - far) % ways * step, axis=0)
+        if 2 * far < ways:
+            going_down = lax.ppermute(going_down, "col", [(d, (d - 1) % ways) for d in range(ways)])
+            full = lax.dynamic_update_slice_in_dim(
+                full, going_down, (here + far) % ways * step, axis=0
+            )
+    whole = full
     token_total = whole.shape[0]
     chosen = whole
     outputs = lax.psum_scatter(

time: 276 us -> 241 us (0.87)
  waiting for transfers between devices: 210 us -> 160 us
  starting transfers between devices: 0.34 us -> 25.8 us
  local copies, waits for them, and re-layouts: 22.8 us -> 15.1 us
  matrix products: 27.2 us -> 23.7 us
    reduce_scatter x0 -> x1, waiting for transfers between devices: none -> 52.4 us  [local(): lax.psum_scatter(jnp.dot(chosen, masked, preferred_element_type=jnp.float...]
    all_gather x1, waiting for transfers between devices: 50.4 us -> 0.02 us  [local(): shard_rows = lax.all_gather(cotangent, 'row', axis=0, tiled=True)]
    unnamed x6 -> x4, waiting for transfers between devices: 124 us -> 81.3 us
    all_gather x1 -> x0, waiting for transfers between devices: 35.6 us -> none  [local(): whole = lax.all_gather(inputs, 'col', axis=0, tiled=True)]
    ppermute x0 -> x15, waiting for transfers between devices: none -> 26.2 us  [the longest x8 26.2 us: local(): lax.ppermute(going_up, 'col', [(d, (d + 1) % ways) for d in range(ways)])]
    ppermute x0 -> x15, starting transfers between devices: none -> 25.6 us  [the longest x7 21.6 us: local(): lax.ppermute(going_down, 'col', [(d, (d - 1) % ways) for d in range(ways)])]
    unnamed x4 -> x11, local copies, waits for them, and re-layouts: 19.4 us -> 10.1 us
    dot_general x1, matrix products: 9.1 us -> 6.15 us  [local(): jnp.dot(chosen, masked, preferred_element_type=jnp.float32)]
  transfers between devices with their start and end apart: 4 -> 18, of which waited for: 4 -> 9; matrix products, arithmetic and copies ran while one was open for 18% -> 16% of each run, Pallas kernels for 0% -> 0%
where the time goes in v1:
time: 241 us; the launch traced here: 239 us
  waiting for transfers between devices  160 us (66%)
  starting transfers between devices  25.8 us (11%)
  matrix products  23.7 us (10%)
  local copies, waits for them, and re-layouts  15.1 us (6%)
  between operations  13.9 us (6%)
    unnamed x4, waiting for transfers between devices  81.3 us
    reduce_scatter x1, waiting for transfers between devices, local(): lax.psum_scatter(jnp.dot(chosen, masked, preferred_element_type=jnp.float...  52.4 us
    ppermute x8, waiting for transfers between devices, local(): lax.ppermute(going_up, 'col', [(d, (d + 1) % ways) for d in range(ways)])  26.2 us
    ppermute x7, starting transfers between devices, local(): lax.ppermute(going_down, 'col', [(d, (d - 1) % ways) for d in range(ways)])  21.6 us
    unnamed x11, local copies, waits for them, and re-layouts  10.1 us
    dot_general x1, matrix products, local(): lax.dot_general(shard_rows, masked, (((1,), (1,)), ((), ())), preferred_e...  8.97 us
    dot_general x1, matrix products, local(): lax.dot_general(chosen, shard_rows, (((0,), (0,)), ((), ())), preferred_e...  8.55 us
    dot_general x1, matrix products, local(): jnp.dot(chosen, masked, preferred_element_type=jnp.float32)  6.15 us
  transfers between devices with their start and end apart: 18, of which 9 were waited for; matrix products, arithmetic and copies ran while one was open for 16% of the time, Pallas kernels for 0%

profile of v1, /device:TPU:10, one launch (start us, length us, event | category | flops | bytes accessed | tf_op | source)
XLA Modules:
  0.0 239.1 jit_solution(10909524214278542966)
XLA Ops:
  7.2 0.7 all-gather.2.cloned.1.call-update
  7.9 1.6 collective-permute-start
  9.5 0.5 collective-permute-start.1
  10.0 0.7 convert_element_type.20
  10.7 0.1 copy.12
  10.8 3.9 %copy.13 = bf16[512,1792]{0,1:T(8,128)(2,1)} copy(bf16[512,1792]{1,0:T(8,128)(2,1)} %param.5) | data formatting | bytes 3670016 | tf_op args[1]
  14.7 0.1 broadcast_in_dim.4
  14.9 1.6 collective-permute-start.2
  16.5 1.3 collective-permute-start.3
  17.8 2.8 %collective-permute-done.2 = bf16[128,512]{1,0:T(8,128)(2,1)S(1)} collective-permute-done((bf16[128,512]{1,0:T(8,128)(2,1)S(1)}, bf16[128,512]{1,0:T(8,128)(2,1)S(1)}, u32[]{:S(2)}, u32[]{:S(2)}) %collective-permute-start.2) | collective-permute-done | bytes 131104 | tf_op jit(solution)/shard_map/ppermute | solution.py:26
  20.6 0.9 collective-permute-start.4
  21.4 3.3 %collective-permute-start.5 = (bf16[128,512]{1,0:T(8,128)(2,1)S(1)}, bf16[128,512]{1,0:T(8,128)(2,1)S(1)}, u32[]{:S(2)}, u32[]{:S(2)}) collective-permute-start(bf16[128,512]{1,0:T(8,128)(2,1)S(1)} %collective-permute-done.3), channel_id=1, source_target_pairs={{0,15},{1,0},{2,1},{3,2},{4,3},{5,4},{6,5},{7,6},{8,7},{9,8},{10,9... | collective-permute-start | bytes 393224 | tf_op jit(solution)/shard_map/ppermute | solution.py:29
  24.7 2.9 %collective-permute-done.4 = bf16[128,512]{1,0:T(8,128)(2,1)S(1)} collective-permute-done((bf16[128,512]{1,0:T(8,128)(2,1)S(1)}, bf16[128,512]{1,0:T(8,128)(2,1)S(1)}, u32[]{:S(2)}, u32[]{:S(2)}) %collective-permute-start.4) | collective-permute-done | bytes 131104 | tf_op jit(solution)/shard_map/ppermute | solution.py:26
  27.6 4.1 %collective-permute-start.7 = (bf16[128,512]{1,0:T(8,128)(2,1)S(1)}, bf16[128,512]{1,0:T(8,128)(2,1)S(1)}, u32[]{:S(2)}, u32[]{:S(2)}) collective-permute-start(bf16[128,512]{1,0:T(8,128)(2,1)S(1)} %collective-permute-done.5), channel_id=1, source_target_pairs={{0,15},{1,0},{2,1},{3,2},{4,3},{5,4},{6,5},{7,6},{8,7},{9,8},{10,9... | collective-permute-start | bytes 393224 | tf_op jit(solution)/shard_map/ppermute | solution.py:29
  31.8 2.9 %collective-permute-done.6 = bf16[128,512]{1,0:T(8,128)(2,1)S(1)} collective-permute-done((bf16[128,512]{1,0:T(8,128)(2,1)S(1)}, bf16[128,512]{1,0:T(8,128)(2,1)S(1)}, u32[]{:S(2)}, u32[]{:S(2)}) %collective-permute-start.6) | collective-permute-done | bytes 131104 | tf_op jit(solution)/shard_map/ppermute | solution.py:26
  34.7 4.1 %collective-permute-start.9 = (bf16[128,512]{1,0:T(8,128)(2,1)S(1)}, bf16[128,512]{1,0:T(8,128)(2,1)S(1)}, u32[]{:S(2)}, u32[]{:S(2)}) collective-permute-start(bf16[128,512]{1,0:T(8,128)(2,1)S(1)} %collective-permute-done.7), channel_id=1, source_target_pairs={{0,15},{1,0},{2,1},{3,2},{4,3},{5,4},{6,5},{7,6},{8,7},{9,8},{10,9... | collective-permute-start | bytes 393224 | tf_op jit(solution)/shard_map/ppermute | solution.py:29
  38.9 3.2 %collective-permute-done.8 = bf16[128,512]{1,0:T(8,128)(2,1)S(1)} collective-permute-done((bf16[128,512]{1,0:T(8,128)(2,1)S(1)}, bf16[128,512]{1,0:T(8,128)(2,1)S(1)}, u32[]{:S(2)}, u32[]{:S(2)}) %collective-permute-start.8) | collective-permute-done | bytes 131104 | tf_op jit(solution)/shard_map/ppermute | solution.py:26
  42.1 4.5 %collective-permute-start.11 = (bf16[128,512]{1,0:T(8,128)(2,1)S(1)}, bf16[128,512]{1,0:T(8,128)(2,1)S(1)}, u32[]{:S(2)}, u32[]{:S(2)}) collective-permute-start(bf16[128,512]{1,0:T(8,128)(2,1)S(1)} %collective-permute-done.9), channel_id=1, source_target_pairs={{0,15},{1,0},{2,1},{3,2},{4,3},{5,4},{6,5},{7,6},{8,7},{9,8},{10,9... | collective-permute-start | bytes 393224 | tf_op jit(solution)/shard_map/ppermute | solution.py:29
  46.6 4.3 %collective-permute-done.10 = bf16[128,512]{1,0:T(8,128)(2,1)S(1)} collective-permute-done((bf16[128,512]{1,0:T(8,128)(2,1)S(1)}, bf16[128,512]{1,0:T(8,128)(2,1)S(1)}, u32[]{:S(2)}, u32[]{:S(2)}) %collective-permute-start.10) | collective-permute-done | bytes 131104 | tf_op jit(solution)/shard_map/ppermute | solution.py:26
  50.9 3.9 %collective-permute-start.13 = (bf16[128,512]{1,0:T(8,128)(2,1)S(1)}, bf16[128,512]{1,0:T(8,128)(2,1)S(1)}, u32[]{:S(2)}, u32[]{:S(2)}) collective-permute-start(bf16[128,512]{1,0:T(8,128)(2,1)S(1)} %collective-permute-done.11), channel_id=1, source_target_pairs={{0,15},{1,0},{2,1},{3,2},{4,3},{5,4},{6,5},{7,6},{8,7},{9,8},{10,9... | collective-permute-start | bytes 393224 | tf_op jit(solution)/shard_map/ppermute | solution.py:29
  54.8 3.4 %collective-permute-done.12 = bf16[128,512]{1,0:T(8,128)(2,1)S(1)} collective-permute-done((bf16[128,512]{1,0:T(8,128)(2,1)S(1)}, bf16[128,512]{1,0:T(8,128)(2,1)S(1)}, u32[]{:S(2)}, u32[]{:S(2)}) %collective-permute-start.12) | collective-permute-done | bytes 131104 | tf_op jit(solution)/shard_map/ppermute | solution.py:26
  58.2 6.7 %collective-permute-done.14 = bf16[128,512]{1,0:T(8,128)(2,1)S(1)} collective-permute-done((bf16[128,512]{1,0:T(8,128)(2,1)S(1)}, bf16[128,512]{1,0:T(8,128)(2,1)S(1)}, u32[]{:S(2)}, u32[]{:S(2)}) %collective-permute-start.14) | collective-permute-done | bytes 131104 | tf_op jit(solution)/shard_map/ppermute | solution.py:26
  65.0 0.5 broadcast_in_dim.10
  65.6 0.8 copy-done
  66.3 6.2 %convolution_convert_fusion = bf16[2048,1792]{1,0:T(8,128)(2,1)} fusion(bf16[2048,512]{1,0:T(8,128)(2,1)S(1)} %constant_dynamic-update-slice_fusion, bf16[512,1792]{0,1:T(8,128)(2,1)S(1)} %copy-done.2, bf16[224,8,4,128]{3,2,1,0:T(4,128)(2,1)S(1)} %bitcast.20), kind=kOutput, calls=%fused_computation | convolution fusion | flops 3762683904 | bytes 13107200 | tf_op jit(solution)/shard_map/dot_general | solution.py:37
  72.6 9.0 %fusion = bf16[2048,512]{0,1:T(8,128)(2,1)} fusion(bf16[2048,1792]{1,0:T(8,128)(2,1)} %all-gather.2.cloned.1.call-done, bf16[512,1792]{0,1:T(8,128)(2,1)} %copy.13, bf16[224,8,4,128]{3,2,1,0:T(4,128)(2,1)S(1)} %bitcast.21), kind=kOutput, calls=%fused_computation.3 | convolution fusion | flops 3760062464 | bytes 13107200 | tf_op jit(solution)/shard_map/dot_general | solution.py:43
  81.6 3.9 %copy.16 = bf16[2048,512]{1,0:T(8,128)(2,1)} copy(bf16[2048,512]{0,1:T(8,128)(2,1)} %fusion) | data formatting | bytes 4194304
  85.5 1.5 copy.26
  87.0 4.0 %copy.14 = bf16[512,1792]{1,0:T(8,128)(2,1)} copy(bf16[512,1792]{0,1:T(8,128)(2,1)} %bitcast.23) | data formatting | bytes 3670016 | tf_op jit(solution)/shard_map/reshape | solution.py:13
  91.1 8.6 %multiply_convert_fusion = bf16[512,1792]{1,0:T(8,128)(2,1)} fusion(bf16[512,1792]{1,0:T(8,128)(2,1)} %copy.14, bf16[2048,512]{1,0:T(8,128)(2,1)S(1)} %copy-done.1, bf16[2048,1792]{1,0:T(8,128)(2,1)} %all-gather.2.cloned.1.call-done), kind=kOutput, calls=%fused_computation.1 | convolution fusion | flops 3761766400 | bytes 13107200 | tf_op jit(solution)/shard_map/dot_general | solution.py:48
  99.6 52.4 %reduce-scatter.5.cloned.1.call-done = bf16[128,1792]{1,0:T(8,128)(2,1)} async-done(((bf16[2048,1792]{1,0:T(8,128)(2,1)}), bf16[128,1792]{1,0:T(8,128)(2,1)}) %reduce-scatter.5.cloned.1.call-update) | async-done | bytes 458768 | tf_op jit(solution)/shard_map/reduce_scatter | solution.py:36
  152.0 80.6 %reduce-scatter.7.cloned.1.call-done = bf16[128,512]{1,0:T(8,128)(2,1)} async-done(((bf16[2048,512]{1,0:T(8,128)(2,1)}), bf16[128,512]{1,0:T(8,128)(2,1)}) %reduce-scatter.7.cloned.1.call-update) | async-done | bytes 131088
  (42 shorter events, 0.5 us)
Async XLA Ops:
  7.2 65.4 %all-gather.2.cloned.1.call-start = ((), (), s32[]{:S(2)}) async-start(), calls=%async_computation.3 | async-start | bytes 7798784 | tf_op jit(solution)/shard_map/all_gather | solution.py:42
  7.9 144.1 %reduce-scatter.5.cloned.1.call-start = ((), (), s32[]{:S(2)}) async-start(), calls=%async_computation.2 | async-start | bytes 7798784 | tf_op jit(solution)/shard_map/reduce_scatter | solution.py:36
  7.9 6.9 %collective-permute-start = (bf16[128,512]{1,0:T(8,128)(2,1)}, bf16[128,512]{1,0:T(8,128)(2,1)S(1)}, u32[]{:S(2)}, u32[]{:S(2)}) collective-permute-start(bf16[128,512]{1,0:T(8,128)(2,1)} %param.4), channel_id=1, source_target_pairs={{0,1},{1,2},{2,3},{3,4},{4,5},{5,6},{6,7},{7,8},{8,9},{9,10},{10,1... | collective-permute-start | bytes 393224 | tf_op jit(solution)/shard_map/ppermute | solution.py:26
  9.5 7.0 %collective-permute-start.1 = (bf16[128,512]{1,0:T(8,128)(2,1)}, bf16[128,512]{1,0:T(8,128)(2,1)S(1)}, u32[]{:S(2)}, u32[]{:S(2)}) collective-permute-start(bf16[128,512]{1,0:T(8,128)(2,1)} %param.4), channel_id=1, source_target_pairs={{0,15},{1,0},{2,1},{3,2},{4,3},{5,4},{6,5},{7,6},{8,7},{9,8},{10,9... | collective-permute-start | bytes 393224 | tf_op jit(solution)/shard_map/ppermute | solution.py:29
  10.8 4.0 %copy-start.3 = (bf16[128,512]{1,0:T(8,128)(2,1)S(1)}, bf16[128,512]{1,0:T(8,128)(2,1)}, u32[]{:S(2)}) copy-start(bf16[128,512]{1,0:T(8,128)(2,1)} %param.4) | copy-start | bytes 393220
  14.9 5.7 %collective-permute-start.2 = (bf16[128,512]{1,0:T(8,128)(2,1)S(1)}, bf16[128,512]{1,0:T(8,128)(2,1)S(1)}, u32[]{:S(2)}, u32[]{:S(2)}) collective-permute-start(bf16[128,512]{1,0:T(8,128)(2,1)S(1)} %collective-permute-done), channel_id=1, source_target_pairs={{0,1},{1,2},{2,3},{3,4},{4,5},{5,6},{6,7},{7,8},{8,9},{9,10},{10,1... | collective-permute-start | bytes 393224 | tf_op jit(solution)/shard_map/ppermute | solution.py:26
  16.5 5.0 %collective-permute-start.3 = (bf16[128,512]{1,0:T(8,128)(2,1)S(1)}, bf16[128,512]{1,0:T(8,128)(2,1)S(1)}, u32[]{:S(2)}, u32[]{:S(2)}) collective-permute-start(bf16[128,512]{1,0:T(8,128)(2,1)S(1)} %collective-permute-done.1), channel_id=1, source_target_pairs={{0,15},{1,0},{2,1},{3,2},{4,3},{5,4},{6,5},{7,6},{8,7},{9,8},{10,9... | collective-permute-start | bytes 393224 | tf_op jit(solution)/shard_map/ppermute | solution.py:29
  20.6 7.1 %collective-permute-start.4 = (bf16[128,512]{1,0:T(8,128)(2,1)S(1)}, bf16[128,512]{1,0:T(8,128)(2,1)S(1)}, u32[]{:S(2)}, u32[]{:S(2)}) collective-permute-start(bf16[128,512]{1,0:T(8,128)(2,1)S(1)} %collective-permute-done.2), channel_id=1, source_target_pairs={{0,1},{1,2},{2,3},{3,4},{4,5},{5,6},{6,7},{7,8},{8,9},{9,10},{10,1... | collective-permute-start | bytes 393224 | tf_op jit(solution)/shard_map/ppermute | solution.py:26
  21.4 6.2 %collective-permute-start.5 = (bf16[128,512]{1,0:T(8,128)(2,1)S(1)}, bf16[128,512]{1,0:T(8,128)(2,1)S(1)}, u32[]{:S(2)}, u32[]{:S(2)}) collective-permute-start(bf16[128,512]{1,0:T(8,128)(2,1)S(1)} %collective-permute-done.3), channel_id=1, source_target_pairs={{0,15},{1,0},{2,1},{3,2},{4,3},{5,4},{6,5},{7,6},{8,7},{9,8},{10,9... | collective-permute-start | bytes 393224 | tf_op jit(solution)/shard_map/ppermute | solution.py:29
  27.6 7.1 %collective-permute-start.6 = (bf16[128,512]{1,0:T(8,128)(2,1)S(1)}, bf16[128,512]{1,0:T(8,128)(2,1)S(1)}, u32[]{:S(2)}, u32[]{:S(2)}) collective-permute-start(bf16[128,512]{1,0:T(8,128)(2,1)S(1)} %collective-permute-done.4), channel_id=1, source_target_pairs={{0,1},{1,2},{2,3},{3,4},{4,5},{5,6},{6,7},{7,8},{8,9},{9,10},{10,1... | collective-permute-start | bytes 393224 | tf_op jit(solution)/shard_map/ppermute | solution.py:26
  27.6 7.1 %collective-permute-start.7 = (bf16[128,512]{1,0:T(8,128)(2,1)S(1)}, bf16[128,512]{1,0:T(8,128)(2,1)S(1)}, u32[]{:S(2)}, u32[]{:S(2)}) collective-permute-start(bf16[128,512]{1,0:T(8,128)(2,1)S(1)} %collective-permute-done.5), channel_id=1, source_target_pairs={{0,15},{1,0},{2,1},{3,2},{4,3},{5,4},{6,5},{7,6},{8,7},{9,8},{10,9... | collective-permute-start | bytes 393224 | tf_op jit(solution)/shard_map/ppermute | solution.py:29
  31.8 34.5 %copy-start.2 = (bf16[512,1792]{0,1:T(8,128)(2,1)S(1)}, bf16[512,1792]{0,1:T(8,128)(2,1)}, u32[]{:S(2)}) copy-start(bf16[512,1792]{0,1:T(8,128)(2,1)} %copy.13) | copy-start | bytes 5505028
  34.7 7.3 %collective-permute-start.8 = (bf16[128,512]{1,0:T(8,128)(2,1)S(1)}, bf16[128,512]{1,0:T(8,128)(2,1)S(1)}, u32[]{:S(2)}, u32[]{:S(2)}) collective-permute-start(bf16[128,512]{1,0:T(8,128)(2,1)S(1)} %collective-permute-done.6), channel_id=1, source_target_pairs={{0,1},{1,2},{2,3},{3,4},{4,5},{5,6},{6,7},{7,8},{8,9},{9,10},{10,1... | collective-permute-start | bytes 393224 | tf_op jit(solution)/shard_map/ppermute | solution.py:26
  34.7 7.3 %collective-permute-start.9 = (bf16[128,512]{1,0:T(8,128)(2,1)S(1)}, bf16[128,512]{1,0:T(8,128)(2,1)S(1)}, u32[]{:S(2)}, u32[]{:S(2)}) collective-permute-start(bf16[128,512]{1,0:T(8,128)(2,1)S(1)} %collective-permute-done.7), channel_id=1, source_target_pairs={{0,15},{1,0},{2,1},{3,2},{4,3},{5,4},{6,5},{7,6},{8,7},{9,8},{10,9... | collective-permute-start | bytes 393224 | tf_op jit(solution)/shard_map/ppermute | solution.py:29
  42.1 8.8 %collective-permute-start.10 = (bf16[128,512]{1,0:T(8,128)(2,1)S(1)}, bf16[128,512]{1,0:T(8,128)(2,1)S(1)}, u32[]{:S(2)}, u32[]{:S(2)}) collective-permute-start(bf16[128,512]{1,0:T(8,128)(2,1)S(1)} %collective-permute-done.8), channel_id=1, source_target_pairs={{0,1},{1,2},{2,3},{3,4},{4,5},{5,6},{6,7},{7,8},{8,9},{9,10},{10,1... | collective-permute-start | bytes 393224 | tf_op jit(solution)/shard_map/ppermute | solution.py:26
  42.1 8.8 %collective-permute-start.11 = (bf16[128,512]{1,0:T(8,128)(2,1)S(1)}, bf16[128,512]{1,0:T(8,128)(2,1)S(1)}, u32[]{:S(2)}, u32[]{:S(2)}) collective-permute-start(bf16[128,512]{1,0:T(8,128)(2,1)S(1)} %collective-permute-done.9), channel_id=1, source_target_pairs={{0,15},{1,0},{2,1},{3,2},{4,3},{5,4},{6,5},{7,6},{8,7},{9,8},{10,9... | collective-permute-start | bytes 393224 | tf_op jit(solution)/shard_map/ppermute | solution.py:29
  50.9 7.3 %collective-permute-start.12 = (bf16[128,512]{1,0:T(8,128)(2,1)S(1)}, bf16[128,512]{1,0:T(8,128)(2,1)S(1)}, u32[]{:S(2)}, u32[]{:S(2)}) collective-permute-start(bf16[128,512]{1,0:T(8,128)(2,1)S(1)} %collective-permute-done.10), channel_id=1, source_target_pairs={{0,1},{1,2},{2,3},{3,4},{4,5},{5,6},{6,7},{7,8},{8,9},{9,10},{10,1... | collective-permute-start | bytes 393224 | tf_op jit(solution)/shard_map/ppermute | solution.py:26
  50.9 7.3 %collective-permute-start.13 = (bf16[128,512]{1,0:T(8,128)(2,1)S(1)}, bf16[128,512]{1,0:T(8,128)(2,1)S(1)}, u32[]{:S(2)}, u32[]{:S(2)}) collective-permute-start(bf16[128,512]{1,0:T(8,128)(2,1)S(1)} %collective-permute-done.11), channel_id=1, source_target_pairs={{0,15},{1,0},{2,1},{3,2},{4,3},{5,4},{6,5},{7,6},{8,7},{9,8},{10,9... | collective-permute-start | bytes 393224 | tf_op jit(solution)/shard_map/ppermute | solution.py:29
  58.2 6.8 %collective-permute-start.14 = (bf16[128,512]{1,0:T(8,128)(2,1)S(1)}, bf16[128,512]{1,0:T(8,128)(2,1)S(1)}, u32[]{:S(2)}, u32[]{:S(2)}) collective-permute-start(bf16[128,512]{1,0:T(8,128)(2,1)S(1)} %collective-permute-done.12), channel_id=1, source_target_pairs={{0,1},{1,2},{2,3},{3,4},{4,5},{5,6},{6,7},{7,8},{8,9},{9,10},{10,1... | collective-permute-start | bytes 393224 | tf_op jit(solution)/shard_map/ppermute | solution.py:26
  65.0 1.3 copy-start
  72.5 160.1 %reduce-scatter.7.cloned.1.call-start = ((), (), s32[]{:S(2)}) async-start(), calls=%async_computation.4 | async-start | bytes 2228224
  87.0 4.0 %copy-start.1 = (bf16[2048,512]{1,0:T(8,128)(2,1)S(1)}, bf16[2048,512]{1,0:T(8,128)(2,1)}, u32[]{:S(2)}) copy-start(bf16[2048,512]{1,0:T(8,128)(2,1)} %copy-done) | copy-start | bytes 6291460
Sparse Core Ops, SparseCore 0:
  9.8 53.8 all-gather.1
  72.6 79.3 reduce-scatter.4
  156.1 76.4 reduce-scatter.6
